TPU v7x, 256 devices: a whole 4x4x8 slice. The times are simulated.
256 devices in a mesh: dp: 8 (over y, core), expert: 32 (over x, z).
Axes of the slice: x: 4, y: 4, z: 8, core: 2. Of those that a mesh axis runs over, the one named last changes fastest.
Arguments:
- tokens: bfloat16 [32768, 3072], P(('dp', 'expert')), may hold values from -6 to 6
- cotangent: bfloat16 [32768, 3072], P(('dp', 'expert')), may hold values from -0.3125 to 0.3125
- route_ids: int32 [32768, 2], P(('dp', 'expert')), may hold values from 0 to 7, all different within a row; in each aligned block of 128 rows (0 to 127, 128 to 255, ...) at most 36 rows name the same one
- route_probs: float32 [32768, 2], P(('dp', 'expert')), may hold values from 0.2 to 1
- gate_weight: bfloat16 [3072, 8192], P(None, 'expert'), may hold values from -0.109375 to 0.109375
- up_weight: bfloat16 [3072, 8192], P(None, 'expert'), may hold values from -0.109375 to 0.109375
- down_weight: bfloat16 [8192, 3072], P('expert'), may hold values from -0.0625 to 0.0625
Outputs:
- token_grad: bfloat16 [32768, 3072], P(('dp', 'expert'))
- gate_grad: bfloat16 [3072, 8192], P('dp', 'expert')
- up_grad: bfloat16 [3072, 8192], P('dp', 'expert')
- down_grad: bfloat16 [8192, 3072], P('expert', 'dp')
Inputs may be any that keep to these rules, and one draw needn't show every extreme that they name: `route_ids`: in every block of 128 consecutive tokens (the tokens of one device) at most 36 tokens name any one expert, a bound that some block reaches; a token's 2 ids differ.
All inputs are finite; a program needn't handle non-finite values.
Results may differ from a plain program's by a relative error of at most 0.023.
Values may be sent and summed in bfloat16 or wider, within the bound.
A program may use at most 128 MiB of HBM per device.

v0:
```python
import functools
import heapq

import jax
import jax.numpy as jnp
from jax import lax
from jax.experimental import pallas as pl
from jax.experimental.pallas import tpu as pltpu
from jax.sharding import PartitionSpec as P

CAP = 36
ROWS = 32
PACK = 8
EXTRA = CAP - ROWS
TOK = 128
D = 3072
H = 256
CA = 1280
CB = D - CA
NX, NZ, NY = 4, 8, 4
SH = D // 8
BF = jnp.bfloat16
F32 = jnp.float32
LINK_RATE = 46e3
CORE_RATE = 250e3
LATENCY = 1.6

REACH = {
    0: {"x": (2, 1), "z": (4, 3)},
    1: {"x": (1, 2), "z": (3, 4)},
}
SIZE = {"x": NX, "z": NZ, "y": NY}
RS_COLS = {
    ("A", 0): (0, CA // 2),
    ("A", 1): (CA // 2, CA // 2),
    ("B", 0): (CA, CB // 2),
    ("B", 1): (CA + CB // 2, CB // 2),
}


class Msg:
    def __init__(self, link, size, src, dst):
        self.link, self.size, self.src, self.dst = link, size, src, dst


class Task:
    def __init__(self, name, deps, sends=(), dur=0.0, rank=0, emit=None):
        self.name, self.deps, self.sends = name, tuple(deps), list(sends)
        self.dur, self.rank, self.emit = dur, rank, emit


GROUP = NX * CAP


def row_of(dz, dx):
    return dz * GROUP + dx * ROWS


def pack_of(dz, dx):
    return (dz * NX + dx) * PACK


def plan():
    msgs, tasks = {}, []

    first_sends, hold = [], []
    by_dz = {dz: [] for dz in range(NZ)}
    for kind, f, g, cols in (("A", "x", "z", CA), ("B", "z", "x", CB)):
        for tw in (0, 1):
            def at(cf, cg):
                dx, dz = (cf, cg) if f == "x" else (cg, cf)
                return dz % NZ, dx % NX

            def send(cf, cg, axis, up):
                step = -1 if up else 1
                nf, ng = (cf + step, cg) if axis == f else (cf, cg + step)
                dst = at(nf, ng)
                link = axis + ("+" if up else "-")
                keys = []
                for what, name, size in (("G", "ag", ROWS * cols), ("E", "age", PACK * cols // 2)):
                    key = (name, kind, tw) + dst
                    msgs[key] = Msg(link, size * 2, (what, kind, tw) + at(cf, cg), (what, kind, tw) + dst)
                    keys.append(key)
                by_dz[dst[0]].extend(keys)
                return keys

            def visit(cf, cg, via, up, hops):
                out = []
                if via in (None, f):
                    for u in (True, False):
                        reach = REACH[tw][f][0 if u else 1]
                        if via is None or (u == up and hops < reach):
                            out.append((send(cf, cg, f, u), cf + (-1 if u else 1), cg, f, u, 1 if via is None else hops + 1))
                    for u in (True, False):
                        out.append((send(cf, cg, g, u), cf, cg + (-1 if u else 1), g, u, 1))
                elif hops < REACH[tw][g][0 if up else 1]:
                    out.append((send(cf, cg, g, up), cf, cg + (-1 if up else 1), g, up, hops + 1))
                if via is None:
                    first_sends.extend(k for o in out for k in o[0])
                elif out:
                    here = (kind, tw) + at(cf, cg)
                    sends = [k for o in out for k in o[0]]
                    tasks.append(Task(("fwd",) + here, [("ag",) + here, ("age",) + here], sends, 0.05, 0))
                    if any(msgs[k].link[0] == "x" for k in sends):
                        hold.append(("fwd",) + here)
                for key, a, b, v, u, h in out:
                    visit(a, b, v, u, h)

            visit(0, 0, None, None, 0)
    tasks.append(Task("pick", [], first_sends, 2.0, 0, ("pick",)))

    for dz in range(NZ):
        tasks.append(Task(("main", dz), ["pick", "weights"] + by_dz[dz], [], 3.0, 3, ("main", dz)))
    tasks.append(Task("weights", ["pick"], [], 0.1, 1, ("weights",)))
    task_of = {t.name: t for t in tasks}

    def chain(kind, tw, axis, up, fixed, at_of, blocks, ready, packed=False):
        c0, cols = RS_COLS[kind, tw]
        what, nrows = "P", ROWS * blocks
        if packed:
            what, nrows, c0, cols = "P" + kind, PACK * blocks, 0, (CA if kind == "A" else CB) // 2
        reach = REACH[tw][axis][0 if up else 1]
        sign = 1 if up else -1
        prev = None
        for k in range(reach, -1, -1):
            here = (sign * k) % SIZE[axis]
            r0 = pack_of(*at_of(here)) if packed else row_of(*at_of(here))
            name = ("rs", kind, tw, axis, up, fixed, packed, k)
            key = ("rsm", kind, tw, axis, up, fixed, packed, k - 1)
            deps = list(ready(here))
            if prev is not None:
                deps.append(prev)
            sends = []
            if k > 0:
                msgs[key] = Msg(
                    axis + ("+" if up else "-"), nrows * cols * 2, (what, r0, nrows, c0, cols), ("R", key, nrows, cols)
                )
                sends = [key]
            emit = None if prev is None else ("add", prev, what, r0, nrows, c0, cols)
            dur = 0.0 if prev is None else 0.1 + nrows * cols * 2 / 1.5e6
            tasks.append(Task(name, deps, sends, dur, 1 if k else 2, emit))
            prev = key
        return name

    ends = []
    for tw, packed in ((0, False), (1, False), (0, True), (1, True)):
        if not (packed and tw == 1):
            za = {
                p: [
                    chain("A", tw, "z", up, p, lambda h, p=p: (h, p), 2, lambda h: [("main", h)], packed)
                    for up in (True, False)
                ]
                for p in (2, 0)
            }
            ends += [
                chain("A", tw, "x", up, 0, lambda h: (0, h), 1, lambda h: za[h // 2 * 2], packed)
                for up in (True, False)
            ]
        if packed and tw == 0:
            continue
        xb = {}
        for dz in (4, 3, 5, 2, 6, 1, 7, 0):
            xb[dz] = [
                chain(
                    "B", tw, "x", up, dz, lambda h, dz=dz: (dz, h), 1, lambda h, dz=dz: [("main", dz)] + hold, packed
                )
                for up in (True, False)
            ]
        ends += [
            chain("B", tw, "z", up, 0, lambda h: (h, 0), 1, lambda h: xb[h], packed)
            for up in (True, False)
        ]
    tasks.append(Task("final", ends, [], 1.5, 5, ("final",)))

    mains = [("main", dz) for dz in range(NZ)]
    tasks.append(Task("turn", mains, [], 1.5, 4, ("turn",)))
    last = "turn"
    for i, (kind, lo, hi) in enumerate((("A", 0, 2), ("A", 2, 5), ("B", 0, 2), ("B", 2, 4), ("B", 4, 7))):
        tasks.append(Task(("grad", i), [last], [], 0.9 * (hi - lo), 4, ("grad", kind, lo, hi)))
        last = ("grad", i)
    for dy in (2, 3, 1, 0):
        key = ("cx", dy)
        msgs[key] = Msg("core", 3 * H * SH * 2, ("W", dy, True, 0, 3 * H), ("CX", dy))
        task_of_last = tasks[-1]
    grad_end = tasks[-1]
    grad_end.sends = [("cx", dy) for dy in (2, 3, 1, 0)]
    for dy in range(NY):
        tasks.append(Task(("cadd", dy), [last, ("cx", dy)], [], 0.6, 2, ("cadd", dy)))
    dp_ends = []
    half = 3 * H // 2
    for tw in (0, 1):
        for up in (True, False):
            reach = REACH[tw]["x"][0 if up else 1]
            prev = None
            for k in range(reach, -1, -1):
                dy = (k if up else -k) % NY
                name = ("y", tw, up, k)
                key = ("ym", tw, up, k - 1)
                deps = [("cadd", dy)] + ([prev] if prev else [])
                sends = []
                if k > 0:
                    msgs[key] = Msg(
                        "y" + ("+" if up else "-"), half * SH * 2, ("W", dy, False, tw * half, half), ("Y", key)
                    )
                    sends = [key]
                emit = None if prev is None else ("yadd", prev, dy, tw * half, half)
                tasks.append(Task(name, deps, sends, 0.0 if prev is None else 0.4, 2, emit))
                prev = key
            dp_ends.append(name)
    tasks.append(Task("wout", dp_ends, [], 1.0, 5, ("wout",)))
    return msgs, schedule(msgs, tasks)


def schedule(msgs, tasks):
    waiting = {i: set(t.deps) for i, t in enumerate(tasks)}
    users = {}
    for i, t in enumerate(tasks):
        for d in t.deps:
            users.setdefault(d, []).append(i)
    ready, arrivals, free, now, order = [], [], {}, 0.0, []
    times = {}

    def satisfy(key):
        for i in users.get(key, ()):
            waiting[i].discard(key)
            if not waiting[i]:
                heapq.heappush(ready, (tasks[i].rank, i))

    for i in range(len(tasks)):
        if not waiting[i]:
            heapq.heappush(ready, (tasks[i].rank, i))
    seq = 0
    while ready or arrivals:
        while arrivals and arrivals[0][0] <= now:
            satisfy(heapq.heappop(arrivals)[2])
        if not ready:
            now = arrivals[0][0]
            continue
        _, i = heapq.heappop(ready)
        t = tasks[i]
        now += t.dur
        order.append(t)
        times[t.name] = now
        for key in t.sends:
            m = msgs[key]
            start = max(now, free.get(m.link, 0.0))
            rate = CORE_RATE if m.link == "core" else LINK_RATE
            free[m.link] = start + m.size / rate
            seq += 1
            heapq.heappush(arrivals, (free[m.link] + LATENCY, seq, key))
        satisfy(t.name)
    if len(order) != len(tasks):
        raise ValueError("stuck")
    plan.times, plan.end = times, now
    return order


MSGS, ORDER = plan()
KEYS = sorted(MSGS, key=repr)
INDEX = {k: i for i, k in enumerate(KEYS)}
R_SLOT, R_COUNT = {}, {}
for _k in KEYS:
    if _k[0] == "rsm":
        _, _, _nr, _nc = MSGS[_k].dst
        R_SLOT[_k] = R_COUNT.get((_nr, _nc), 0)
        R_COUNT[_nr, _nc] = R_SLOT[_k] + 1
R_SHAPES = sorted(R_COUNT)
Y_KEYS = [k for k in KEYS if k[0] == "ym"]


def kernel(ids, probs, tokens, cot, wg_hbm, wu_hbm, wd_hbm, ret_out, across_out, w_out,
           ga0, ga1, gb0, gb1, ea0, ea1, eb0, eb1, part, pa, pb, wg, wu, wd, gback, uback, hid, turned, w3, cx, yr, *rest):
    landing = dict(zip(R_SHAPES, rest[: len(R_SHAPES)]))
    wsem, send_sem, recv_sem = rest[len(R_SHAPES):]
    gathered = {("A", 0): ga0, ("A", 1): ga1, ("B", 0): gb0, ("B", 1): gb1}
    extras = {("A", 0): ea0, ("A", 1): ea1, ("B", 0): eb0, ("B", 1): eb1}
    sums = {"P": part, "PA": pa, "PB": pb}

    e = lax.axis_index("expert")
    d = lax.axis_index("dp")
    x, z, y, c = e // NZ, e % NZ, d // 2, d % 2
    peer = {
        "z+": {"expert": x * NZ + (z + 1) % NZ},
        "z-": {"expert": x * NZ + (z + NZ - 1) % NZ},
        "x+": {"expert": ((x + 1) % NX) * NZ + z},
        "x-": {"expert": ((x + NX - 1) % NX) * NZ + z},
        "y+": {"dp": ((y + 1) % NY) * 2 + c},
        "y-": {"dp": ((y + NY - 1) % NY) * 2 + c},
        "core": {"dp": y * 2 + 1 - c},
    }
    loads = [
        pltpu.make_async_copy(src, dst, wsem.at[i])
        for i, (src, dst) in enumerate(((wg_hbm, wg), (wu_hbm, wu), (wd_hbm, wd)))
    ]
    for load in loads:
        load.start()
    barrier = pltpu.get_barrier_semaphore()
    for target in peer.values():
        pl.semaphore_signal(barrier, inc=1, device_id=target, device_id_type=pl.DeviceIdType.MESH)

    def shard(dy, other):
        owner = ((y + dy) % NY) * 2 + (1 - c if other else c)
        return pl.ds(pl.multiple_of(owner * SH, 128), SH)

    def ref_of(place):
        what = place[0]
        if what == "G":
            _, kind, tw, dz, dx = place
            return gathered[kind, tw].at[pl.ds(row_of(dz, dx), ROWS), :]
        if what == "E":
            _, kind, tw, dz, dx = place
            return extras[kind, tw].at[pl.ds(pack_of(dz, dx), PACK), :]
        if what in sums:
            _, r0, nr, c0, nc = place
            return sums[what].at[pl.ds(r0, nr), pl.ds(c0, nc)]
        if what == "R":
            _, key, nr, nc = place
            return landing[nr, nc].at[R_SLOT[key]]
        if what == "W":
            _, dy, other, r0, nr = place
            return w3.at[pl.ds(r0, nr), shard(dy, other)]
        if what == "CX":
            return cx.at[place[1]]
        return yr.at[Y_KEYS.index(place[1])]

    copies = {}

    def copy_of(key):
        if key not in copies:
            m = MSGS[key]
            copies[key] = pltpu.make_async_remote_copy(
                src_ref=ref_of(m.src),
                dst_ref=ref_of(m.dst),
                send_sem=send_sem.at[INDEX[key]],
                recv_sem=recv_sem.at[INDEX[key]],
                device_id=peer[m.link],
                device_id_type=pl.DeviceIdType.MESH,
            )
        return copies[key]

    def pick():
        hits = ids[...] == 0
        chosen = jnp.sum(jnp.where(hits, 1.0, 0.0), axis=0, keepdims=True)
        share = jnp.sum(jnp.where(hits, probs[...], 0.0), axis=0, keepdims=True)
        above = lax.broadcasted_iota(jnp.int32, (TOK, TOK), 0) < lax.broadcasted_iota(jnp.int32, (TOK, TOK), 1)
        wide = jnp.broadcast_to(chosen, (TOK, TOK))
        slot = jnp.dot(
            wide.astype(BF), jnp.where(above, 1.0, 0.0).astype(BF), preferred_element_type=F32
        )
        row = lax.broadcasted_iota(jnp.int32, (TOK, TOK), 0).astype(F32)
        whole = jnp.where((slot == row) & (wide > 0.5), 1.0, 0.0)
        across_out[...] = whole[: ROWS + PACK].astype(BF)
        low = whole[ROWS : ROWS + PACK]
        r8 = lax.broadcasted_iota(jnp.int32, (PACK, TOK), 0)
        wanted = (r8 + (ROWS - EXTRA)).astype(F32)
        high = jnp.where((slot[:PACK] == wanted) & (wide[:PACK] > 0.5) & (r8 >= EXTRA), 1.0, 0.0)
        maps = [whole[:ROWS], low, high]
        shares = [jnp.sum(m * share, axis=1, keepdims=True) for m in maps]
        maps = [m.astype(BF) for m in maps]

        def take(k, source, c0, cols, scale):
            got = jnp.dot(maps[k], source[:, pl.ds(c0, cols)], preferred_element_type=F32)
            return got * shares[k] if scale else got

        for c0, cols, kind in ((0, CA, "A"), (CA, CB, "B")):
            for tw, source in ((0, tokens), (1, cot)):
                gathered[kind, tw][pl.ds(0, ROWS), :] = take(0, source, c0, cols, tw == 1).astype(BF)
                extras[kind, tw][pl.ds(0, PACK), :] = (
                    take(1, source, c0, cols // 2, tw == 1) + take(2, source, c0 + cols // 2, cols // 2, tw == 1)
                ).astype(BF)
        pl.semaphore_wait(barrier, len(peer))

    def spread(high, shape, axis):
        i = lax.broadcasted_iota(jnp.int32, shape, axis)
        j = lax.broadcasted_iota(jnp.int32, shape, 1 - axis)
        return jnp.where((i >> 2) * PACK + (i & 3) + (EXTRA if high else 0) == j, 1.0, 0.0).astype(BF)

    def weights():
        for load in loads:
            load.wait()

    nt = (((1,), (1,)), ((), ()))

    def main(dz):
        rows = pl.ds(row_of(dz, 0), GROUP)
        tail = pl.ds(row_of(dz, 0) + NX * ROWS, NX * EXTRA)
        packed = pl.ds(pack_of(dz, 0), NX * PACK)
        for kind, cols in (("A", CA // 2), ("B", CB // 2)):
            for tw in (0, 1):
                for high in (0, 1):
                    gathered[kind, tw][tail, pl.ds(high * cols, cols)] = jnp.dot(
                        spread(high, (NX * EXTRA, NX * PACK), 0), extras[kind, tw][packed, :],
                        preferred_element_type=F32,
                    ).astype(BF)
        ra, rb, sa, sb = ga0[rows, :], gb0[rows, :], ga1[rows, :], gb1[rows, :]
        gate = jnp.dot(ra, wg[pl.ds(0, CA), :], preferred_element_type=F32) + jnp.dot(
            rb, wg[pl.ds(CA, CB), :], preferred_element_type=F32
        )
        up = jnp.dot(ra, wu[pl.ds(0, CA), :], preferred_element_type=F32) + jnp.dot(
            rb, wu[pl.ds(CA, CB), :], preferred_element_type=F32
        )
        back = lax.dot_general(sa, wd[:, pl.ds(0, CA)], nt, preferred_element_type=F32) + lax.dot_general(
            sb, wd[:, pl.ds(CA, CB)], nt, preferred_element_type=F32
        )
        sigma = jax.nn.sigmoid(gate)
        act = gate * sigma
        hid[rows, :] = (act * up).astype(BF)
        gb = (back * up * sigma * (1.0 + gate * (1.0 - sigma))).astype(BF)
        ub = (back * act).astype(BF)
        gback[rows, :] = gb
        uback[rows, :] = ub
        for c0 in range(0, D, 256):
            cols = pl.ds(c0, 256)
            part[rows, cols] = (
                lax.dot_general(gb, wg[cols, :], nt, preferred_element_type=F32)
                + lax.dot_general(ub, wu[cols, :], nt, preferred_element_type=F32)
            ).astype(BF)

        for out, c0, cols in ((pa, 0, CA // 2), (pb, CA, CB // 2)):
            out[packed, :] = sum(
                jnp.dot(
                    spread(high, (NX * PACK, NX * EXTRA), 1), part[tail, pl.ds(c0 + high * cols, cols)],
                    preferred_element_type=F32,
                )
                for high in (0, 1)
            ).astype(BF)

    def add(key, what, r0, nr, c0, nc):
        got = landing[nr, nc].at[R_SLOT[key]]
        here = (pl.ds(r0, nr), pl.ds(c0, nc))
        sums[what][here] = sums[what][here] + got[...]

    def turn():
        turned[pl.ds(0, H), :] = jnp.transpose(gback[...])
        turned[pl.ds(H, H), :] = jnp.transpose(uback[...])
        turned[pl.ds(2 * H, H), :] = jnp.transpose(hid[...])

    def grad(kind, lo, hi):
        base = 0 if kind == "A" else CA
        first, second = gathered[kind, 0], gathered[kind, 1]

        @pl.loop(lo, hi)
        def _(i):
            cols = pl.ds(pl.multiple_of(i * 256, 256), 256)
            out = pl.ds(pl.multiple_of(base + i * 256, 256), 256)
            w3[pl.ds(0, 2 * H), out] = jnp.dot(
                turned[pl.ds(0, 2 * H), :], first[:, cols], preferred_element_type=F32
            ).astype(BF)
            w3[pl.ds(2 * H, H), out] = jnp.dot(
                turned[pl.ds(2 * H, H), :], second[:, cols], preferred_element_type=F32
            ).astype(BF)

    def cadd(dy):
        here = shard(dy, False)
        w3[:, here] = w3[:, here] + cx[dy]

    def yadd(key, dy, r0, nr):
        here = (pl.ds(r0, nr), shard(dy, False))
        w3[here] = w3[here] + yr[Y_KEYS.index(key)]

    def final():
        ret_out[pl.ds(0, ROWS), :] = part[pl.ds(0, ROWS), :]
        for packed, c0, cols in ((pa, 0, CA // 2), (pb, CA, CB // 2)):
            for high in (0, 1):
                ret_out[pl.ds(ROWS, PACK), pl.ds(c0 + high * cols, cols)] = jnp.dot(
                    spread(high, (PACK, NX * PACK), 0), packed[pl.ds(0, NX * PACK), :],
                    preferred_element_type=F32,
                ).astype(BF)

    def wout():
        w_out[...] = w3[:, shard(0, False)]

    run = dict(pick=pick, weights=weights, main=main, add=add, turn=turn, grad=grad,
               cadd=cadd, yadd=yadd, final=final, wout=wout)
    arrived = set()
    for task in ORDER:
        for dep in task.deps:
            if dep in MSGS and dep not in arrived:
                copy_of(dep).wait_recv()
                arrived.add(dep)
        if task.emit is not None:
            run[task.emit[0]](*task.emit[1:])
        for key in task.sends:
            copy_of(key).start()
    for key in KEYS:
        copy_of(key).wait_send()


def per_device(tokens, cotangent, route_ids, route_probs, gate_weight, up_weight, down_weight):
    vmem = pl.BlockSpec(memory_space=pltpu.VMEM)
    anywhere = pl.BlockSpec(memory_space=pl.ANY)
    rows, packs = NZ * GROUP, NZ * NX * PACK
    scratch = [
        pltpu.VMEM((rows, CA), BF), pltpu.VMEM((rows, CA), BF),
        pltpu.VMEM((rows, CB), BF), pltpu.VMEM((rows, CB), BF),
        pltpu.VMEM((packs, CA // 2), BF), pltpu.VMEM((packs, CA // 2), BF),
        pltpu.VMEM((packs, CB // 2), BF), pltpu.VMEM((packs, CB // 2), BF),
        pltpu.VMEM((rows, D), BF),
        pltpu.VMEM((packs, CA // 2), BF), pltpu.VMEM((packs, CB // 2), BF),
        pltpu.VMEM((D, H), BF), pltpu.VMEM((D, H), BF), pltpu.VMEM((H, D), BF),
        pltpu.VMEM((rows, H), BF), pltpu.VMEM((rows, H), BF), pltpu.VMEM((rows, H), BF),
        pltpu.VMEM((3 * H, rows), BF),
        pltpu.VMEM((3 * H, D), BF),
        pltpu.VMEM((NY, 3 * H, SH), BF),
        pltpu.VMEM((len(Y_KEYS), 3 * H // 2, SH), BF),
    ]
    scratch += [pltpu.VMEM((R_COUNT[s],) + s, BF) for s in R_SHAPES]
    scratch += [
        pltpu.SemaphoreType.DMA((3,)),
        pltpu.SemaphoreType.DMA((len(KEYS),)),
        pltpu.SemaphoreType.DMA((len(KEYS),)),
    ]
    returned, across, grads = pl.pallas_call(
        kernel,
        out_shape=(
            jax.ShapeDtypeStruct((ROWS + PACK, D), BF),
            jax.ShapeDtypeStruct((ROWS + PACK, TOK), BF),
            jax.ShapeDtypeStruct((3 * H, SH), BF),
        ),
        in_specs=[vmem, vmem, vmem, vmem, anywhere, anywhere, anywhere],
        out_specs=(vmem, vmem, vmem),
        scratch_shapes=scratch,
        compiler_params=pltpu.CompilerParams(
            collective_id=0, has_side_effects=True, vmem_limit_bytes=67043328
        ),
    )(route_ids.T, route_probs.T, tokens, cotangent, gate_weight, up_weight, down_weight)
    token_grad = lax.dot_general(
        across, returned, (((0,), (0,)), ((), ())), preferred_element_type=F32
    ).astype(BF)
    return token_grad, grads[:H].T, grads[H : 2 * H].T, grads[2 * H :]


def solution(mesh):
    in_specs = (
        P(("dp", "expert"), None),
        P(("dp", "expert"), None),
        P(("dp", "expert"), None),
        P(("dp", "expert"), None),
        P(None, "expert"),
        P(None, "expert"),
        P("expert", None),
    )
    out_specs = (P(("dp", "expert"), None), P("dp", "expert"), P("dp", "expert"), P("expert", "dp"))
    return jax.shard_map(
        per_device, mesh=mesh, in_specs=in_specs, out_specs=out_specs, check_vma=False
    )
```

profile of v0, /device:TPU:2, one launch (start us, length us, event | category | flops | bytes accessed | tf_op | source)
XLA Modules:
  0.0 155.5 jit_solution(8024816810478395355)
XLA Ops:
  0.6 150.1 %shard_map.102 = (bf16[40,3072]{1,0:T(8,128)(2,1)}, bf16[40,128]{1,0:T(8,128)(2,1)}, bf16[768,384]{1,0:T(8,128)(2,1)}) custom-call(s32[2,128]{1,0:T(2,128)} %bitcast.8, f32[2,128]{1,0:T(2,128)} %bitcast.9, bf16[128,3072]{1,0:T(8,128)(2,1)} %tokens.1, bf16[128,3072]{1,0:T(8,128)(2,1)} %cot.1, bf16[3072,256]{1,0:T(8,128)(2,1)} %wg_hbm.1, ...), custom_call_target="tpu_custom_call" | custom-call | tf_op jit(solution)/shard_map/pallas_call | solution.py:513
  150.7 0.0 copy-start
  150.7 0.0 copy-start.1
  150.7 1.9 %fusion = (bf16[256,384]{1,0:T(8,128)(2,1)}, bf16[384,256]{0,1:T(8,128)(2,1)S(1)}, bf16[384,256]{0,1:T(8,128)(2,1)S(1)}) fusion(bf16[768,384]{1,0:T(8,128)(2,1)} %get-tuple-element.9), kind=kLoop, calls=%fused_computation.3 | loop fusion | bytes 1179648 | tf_op jit(solution)/shard_map/slice | solution.py:530
  152.6 0.8 copy.11
  153.4 0.8 copy.12
  154.3 0.0 copy-done
  154.3 0.0 copy-done.1
  154.3 1.3 convolution_convert_fusion
Async XLA Ops:
  150.7 3.6 %copy-start = (bf16[40,3072]{1,0:T(8,128)(2,1)S(1)}, bf16[40,3072]{1,0:T(8,128)(2,1)}, u32[]{:S(2)}) copy-start(bf16[40,3072]{1,0:T(8,128)(2,1)} %get-tuple-element.8) | copy-start | bytes 737284
  150.7 3.6 %copy-start.1 = (bf16[40,128]{1,0:T(8,128)(2,1)S(1)}, bf16[40,128]{1,0:T(8,128)(2,1)}, u32[]{:S(2)}) copy-start(bf16[40,128]{1,0:T(8,128)(2,1)} %get-tuple-element.7) | copy-start | bytes 30724
where the time goes:
time: 156 us
  Pallas kernels  150 us (96%)
  local copies, waits for them, and re-layouts  3.54 us (2%)
    pallas_call x1, Pallas kernels, per_device(): pl.pallas_call(kernel, out_shape=(jax.ShapeDtypeStruct((ROWS + PACK, D),...  150 us

commit v1 on v0

--- a/solution.py
+++ b/solution.py
@@ -19,6 +19,7 @@
 CB = D - CA
 NX, NZ, NY = 4, 8, 4
 SH = D // 8
+UNITS = ((0, 2 * H), (2 * H, H))
 BF = jnp.bfloat16
 F32 = jnp.float32
 LINK_RATE = 46e3
@@ -52,8 +53,12 @@
 GROUP = NX * CAP
 
 
+PLACE = {dz: i for i, dz in enumerate((0, 1, 7, 2, 6, 3, 5, 4))}
+EARLY = 5
+
+
 def row_of(dz, dx):
-    return dz * GROUP + dx * ROWS
+    return PLACE[dz] * GROUP + dx * ROWS
 
 
 def pack_of(dz, dx):
@@ -142,6 +147,7 @@
             prev = key
         return name
 
+    later = {dz: [("main", 4)] if dz in (0, 1, 7) else [] for dz in range(NZ)}
     ends = []
     for tw, packed in ((0, False), (1, False), (0, True), (1, True)):
         if not (packed and tw == 1):
@@ -162,7 +168,7 @@
         for dz in (4, 3, 5, 2, 6, 1, 7, 0):
             xb[dz] = [
                 chain(
-                    "B", tw, "x", up, dz, lambda h, dz=dz: (dz, h), 1, lambda h, dz=dz: [("main", dz)] + hold, packed
+                    "B", tw, "x", up, dz, lambda h, dz=dz: (dz, h), 1, lambda h, dz=dz: [("main", dz)] + hold + later[dz], packed
                 )
                 for up in (True, False)
             ]
@@ -173,41 +179,47 @@
     tasks.append(Task("final", ends, [], 1.5, 5, ("final",)))
 
     mains = [("main", dz) for dz in range(NZ)]
-    tasks.append(Task("turn", mains, [], 1.5, 4, ("turn",)))
-    last = "turn"
-    for i, (kind, lo, hi) in enumerate((("A", 0, 2), ("A", 2, 5), ("B", 0, 2), ("B", 2, 4), ("B", 4, 7))):
-        tasks.append(Task(("grad", i), [last], [], 0.9 * (hi - lo), 4, ("grad", kind, lo, hi)))
-        last = ("grad", i)
-    for dy in (2, 3, 1, 0):
-        key = ("cx", dy)
-        msgs[key] = Msg("core", 3 * H * SH * 2, ("W", dy, True, 0, 3 * H), ("CX", dy))
-        task_of_last = tasks[-1]
-    grad_end = tasks[-1]
-    grad_end.sends = [("cx", dy) for dy in (2, 3, 1, 0)]
-    for dy in range(NY):
-        tasks.append(Task(("cadd", dy), [last, ("cx", dy)], [], 0.6, 2, ("cadd", dy)))
-    dp_ends = []
-    half = 3 * H // 2
-    for tw in (0, 1):
-        for up in (True, False):
-            reach = REACH[tw]["x"][0 if up else 1]
-            prev = None
-            for k in range(reach, -1, -1):
-                dy = (k if up else -k) % NY
-                name = ("y", tw, up, k)
-                key = ("ym", tw, up, k - 1)
-                deps = [("cadd", dy)] + ([prev] if prev else [])
-                sends = []
-                if k > 0:
-                    msgs[key] = Msg(
-                        "y" + ("+" if up else "-"), half * SH * 2, ("W", dy, False, tw * half, half), ("Y", key)
-                    )
-                    sends = [key]
-                emit = None if prev is None else ("yadd", prev, dy, tw * half, half)
-                tasks.append(Task(name, deps, sends, 0.0 if prev is None else 0.4, 2, emit))
-                prev = key
-            dp_ends.append(name)
-    tasks.append(Task("wout", dp_ends, [], 1.0, 5, ("wout",)))
+    tasks.append(Task("turn early", [("main", dz) for dz in PLACE if PLACE[dz] < EARLY], [], 1.0, 4, ("turn", 0)))
+    early = "turn early"
+    for u, (r0, nrows) in enumerate(UNITS):
+        for kind, count in (("A", CA // 256), ("B", CB // 256)):
+            for i in range(count):
+                tasks.append(Task(("early", u, kind, i), [early], [], 0.1 + nrows / 1200, 4, ("early", u, kind, i)))
+                early = tasks[-1].name
+    tasks.append(Task("turn", mains + [early], [], 0.7, 4, ("turn", 1)))
+    last, dp_ends = "turn", []
+    for u, (r0, nrows) in enumerate(UNITS):
+        for kind, count in (("A", CA // 256), ("B", CB // 256)):
+            for i in range(count):
+                tasks.append(Task(("grad", u, kind, i), [last], [], 0.1 + nrows / 1500, 4, ("grad", u, kind, i)))
+                last = tasks[-1].name
+        for dy in (2, 3, 1, 0):
+            msgs["cx", u, dy] = Msg("core", nrows * SH * 2, ("W", dy, True, r0, nrows), ("CX", dy, r0, nrows))
+            tasks[-1].sends.append(("cx", u, dy))
+        for dy in (2, 3, 1, 0):
+            tasks.append(Task(("cadd", u, dy), [last, ("cx", u, dy)], [], 0.1 + nrows / 1500, 2, ("cadd", dy, r0, nrows)))
+        half = nrows // 2
+        for tw in (0, 1):
+            for up in (True, False):
+                reach = REACH[tw]["x"][0 if up else 1]
+                prev = None
+                for k in range(reach, -1, -1):
+                    dy = (k if up else -k) % NY
+                    name = ("y", u, tw, up, k)
+                    key = ("ym", u, tw, up, k - 1)
+                    place = (dy, r0 + tw * half, half)
+                    deps = [("cadd", u, dy)] + ([prev] if prev else [])
+                    sends = []
+                    if k > 0:
+                        msgs[key] = Msg(
+                            "y" + ("+" if up else "-"), half * SH * 2, ("W", dy, False) + place[1:], ("Y", key)
+                        )
+                        sends = [key]
+                    emit = None if prev is None else ("yadd", prev) + place
+                    tasks.append(Task(name, deps, sends, 0.0 if prev is None else 0.1 + half / 1500, 2, emit))
+                    prev = key
+                dp_ends.append(name)
+    tasks.append(Task("wout", dp_ends, [], 0.3, 5, ("wout",)))
     return msgs, schedule(msgs, tasks)
 
 
@@ -217,6 +229,20 @@
     for i, t in enumerate(tasks):
         for d in t.deps:
             users.setdefault(d, []).append(i)
+    tail = {}
+
+    def tail_of(key):
+        if key not in tail:
+            tail[key] = 0.0
+            for i in users.get(key, ()):
+                t = tasks[i]
+                sent = max([msgs[k].size / LINK_RATE + LATENCY + tail_of(k) for k in t.sends], default=0.0)
+                tail[key] = max(tail[key], t.dur + max(sent, tail_of(t.name)))
+        return tail[key]
+
+    for t in tasks:
+        sent = max([msgs[k].size / LINK_RATE + LATENCY + tail_of(k) for k in t.sends], default=0.0)
+        t.tail = max(sent, tail_of(t.name))
     ready, arrivals, free, now, order = [], [], {}, 0.0, []
     times = {}
 
@@ -224,11 +250,11 @@
         for i in users.get(key, ()):
             waiting[i].discard(key)
             if not waiting[i]:
-                heapq.heappush(ready, (tasks[i].rank, i))
+                heapq.heappush(ready, (tasks[i].rank, -tasks[i].tail, i))
 
     for i in range(len(tasks)):
         if not waiting[i]:
-            heapq.heappush(ready, (tasks[i].rank, i))
+            heapq.heappush(ready, (tasks[i].rank, -tasks[i].tail, i))
     seq = 0
     while ready or arrivals:
         while arrivals and arrivals[0][0] <= now:
@@ -236,7 +262,7 @@
         if not ready:
             now = arrivals[0][0]
             continue
-        _, i = heapq.heappop(ready)
+        i = heapq.heappop(ready)[2]
         t = tasks[i]
         now += t.dur
         order.append(t)
@@ -265,15 +291,19 @@
         R_SLOT[_k] = R_COUNT.get((_nr, _nc), 0)
         R_COUNT[_nr, _nc] = R_SLOT[_k] + 1
 R_SHAPES = sorted(R_COUNT)
-Y_KEYS = [k for k in KEYS if k[0] == "ym"]
-
-
-def kernel(ids, probs, tokens, cot, wg_hbm, wu_hbm, wd_hbm, ret_out, across_out, w_out,
-           ga0, ga1, gb0, gb1, ea0, ea1, eb0, eb1, part, pa, pb, wg, wu, wd, gback, uback, hid, turned, w3, cx, yr, *rest):
+Y_SLOT = {}
+for _k in KEYS:
+    if _k[0] == "ym":
+        Y_SLOT[_k] = sum(o[1] == _k[1] for o in Y_SLOT)
+
+
+def kernel(ids, probs, tokens, cot, wg_hbm, wu_hbm, wd_hbm, ret_out, across_out, g_out, u_out, d_out,
+           ga0, ga1, gb0, gb1, ea0, ea1, eb0, eb1, part, pa, pb, wg, wu, wd, gback, uback, hid, turned0, turned1, acc, w3, cx, yr0, yr1, *rest):
     landing = dict(zip(R_SHAPES, rest[: len(R_SHAPES)]))
     wsem, send_sem, recv_sem = rest[len(R_SHAPES):]
     gathered = {("A", 0): ga0, ("A", 1): ga1, ("B", 0): gb0, ("B", 1): gb1}
     extras = {("A", 0): ea0, ("A", 1): ea1, ("B", 0): eb0, ("B", 1): eb1}
+    yr = (yr0, yr1)
     sums = {"P": part, "PA": pa, "PB": pb}
 
     e = lax.axis_index("expert")
@@ -320,8 +350,9 @@
             _, dy, other, r0, nr = place
             return w3.at[pl.ds(r0, nr), shard(dy, other)]
         if what == "CX":
-            return cx.at[place[1]]
-        return yr.at[Y_KEYS.index(place[1])]
+            _, dy, r0, nr = place
+            return cx.at[dy, pl.ds(r0, nr), :]
+        return yr[place[1][1]].at[Y_SLOT[place[1]]]
 
     copies = {}
 
@@ -430,33 +461,38 @@
         here = (pl.ds(r0, nr), pl.ds(c0, nc))
         sums[what][here] = sums[what][here] + got[...]
 
-    def turn():
-        turned[pl.ds(0, H), :] = jnp.transpose(gback[...])
-        turned[pl.ds(H, H), :] = jnp.transpose(uback[...])
-        turned[pl.ds(2 * H, H), :] = jnp.transpose(hid[...])
-
-    def grad(kind, lo, hi):
-        base = 0 if kind == "A" else CA
-        first, second = gathered[kind, 0], gathered[kind, 1]
-
-        @pl.loop(lo, hi)
-        def _(i):
-            cols = pl.ds(pl.multiple_of(i * 256, 256), 256)
-            out = pl.ds(pl.multiple_of(base + i * 256, 256), 256)
-            w3[pl.ds(0, 2 * H), out] = jnp.dot(
-                turned[pl.ds(0, 2 * H), :], first[:, cols], preferred_element_type=F32
-            ).astype(BF)
-            w3[pl.ds(2 * H, H), out] = jnp.dot(
-                turned[pl.ds(2 * H, H), :], second[:, cols], preferred_element_type=F32
-            ).astype(BF)
-
-    def cadd(dy):
-        here = shard(dy, False)
-        w3[:, here] = w3[:, here] + cx[dy]
+    cut = EARLY * GROUP
+    halves = ((0, cut), (cut, NZ * GROUP - cut))
+
+    def turn(late):
+        rows = pl.ds(*halves[late])
+        for i, source in enumerate((gback, uback, hid)):
+            (turned1 if late else turned0)[pl.ds(i * H, H), :] = jnp.transpose(source[rows, :])
+
+    def product(u, kind, i, late):
+        return jnp.dot(
+            (turned1 if late else turned0)[pl.ds(*UNITS[u]), :],
+            gathered[kind, u][pl.ds(*halves[late]), pl.ds(i * 256, 256)],
+            preferred_element_type=F32,
+        )
+
+    def tile(u, kind, i):
+        return pl.ds(*UNITS[u]), pl.ds((0 if kind == "A" else CA) + i * 256, 256)
+
+    def early(u, kind, i):
+        acc[tile(u, kind, i)] = product(u, kind, i, 0)
+
+    def grad(u, kind, i):
+        here = tile(u, kind, i)
+        w3[here] = (acc[here] + product(u, kind, i, 1)).astype(BF)
+
+    def cadd(dy, r0, nr):
+        here = (pl.ds(r0, nr), shard(dy, False))
+        w3[here] = w3[here] + cx[dy, pl.ds(r0, nr), :]
 
     def yadd(key, dy, r0, nr):
         here = (pl.ds(r0, nr), shard(dy, False))
-        w3[here] = w3[here] + yr[Y_KEYS.index(key)]
+        w3[here] = w3[here] + yr[key[1]][Y_SLOT[key]]
 
     def final():
         ret_out[pl.ds(0, ROWS), :] = part[pl.ds(0, ROWS), :]
@@ -468,9 +504,11 @@
                 ).astype(BF)
 
     def wout():
-        w_out[...] = w3[:, shard(0, False)]
-
-    run = dict(pick=pick, weights=weights, main=main, add=add, turn=turn, grad=grad,
+        own = shard(0, False)
+        for i, out in enumerate((g_out, u_out, d_out)):
+            out[...] = w3[pl.ds(i * H, H), own]
+
+    run = dict(early=early, pick=pick, weights=weights, main=main, add=add, turn=turn, grad=grad,
                cadd=cadd, yadd=yadd, final=final, wout=wout)
     arrived = set()
     for task in ORDER:
@@ -499,10 +537,11 @@
         pltpu.VMEM((packs, CA // 2), BF), pltpu.VMEM((packs, CB // 2), BF),
         pltpu.VMEM((D, H), BF), pltpu.VMEM((D, H), BF), pltpu.VMEM((H, D), BF),
         pltpu.VMEM((rows, H), BF), pltpu.VMEM((rows, H), BF), pltpu.VMEM((rows, H), BF),
-        pltpu.VMEM((3 * H, rows), BF),
+        pltpu.VMEM((3 * H, EARLY * GROUP), BF), pltpu.VMEM((3 * H, rows - EARLY * GROUP), BF),
+        pltpu.VMEM((3 * H, D), F32),
         pltpu.VMEM((3 * H, D), BF),
         pltpu.VMEM((NY, 3 * H, SH), BF),
-        pltpu.VMEM((len(Y_KEYS), 3 * H // 2, SH), BF),
+        *(pltpu.VMEM((len(Y_SLOT) // 2, nrows // 2, SH), BF) for _, nrows in UNITS),
     ]
     scratch += [pltpu.VMEM((R_COUNT[s],) + s, BF) for s in R_SHAPES]
     scratch += [
@@ -510,15 +549,15 @@
         pltpu.SemaphoreType.DMA((len(KEYS),)),
         pltpu.SemaphoreType.DMA((len(KEYS),)),
     ]
-    returned, across, grads = pl.pallas_call(
+    returned, across, gate_grad, up_grad, down_grad = pl.pallas_call(
         kernel,
         out_shape=(
             jax.ShapeDtypeStruct((ROWS + PACK, D), BF),
             jax.ShapeDtypeStruct((ROWS + PACK, TOK), BF),
-            jax.ShapeDtypeStruct((3 * H, SH), BF),
+            *(jax.ShapeDtypeStruct((H, SH), BF) for _ in range(3)),
         ),
         in_specs=[vmem, vmem, vmem, vmem, anywhere, anywhere, anywhere],
-        out_specs=(vmem, vmem, vmem),
+        out_specs=(vmem,) * 5,
         scratch_shapes=scratch,
         compiler_params=pltpu.CompilerParams(
             collective_id=0, has_side_effects=True, vmem_limit_bytes=67043328
@@ -527,7 +566,7 @@
     token_grad = lax.dot_general(
         across, returned, (((0,), (0,)), ((), ())), preferred_element_type=F32
     ).astype(BF)
-    return token_grad, grads[:H].T, grads[H : 2 * H].T, grads[2 * H :]
+    return token_grad, gate_grad.T, up_grad.T, down_grad
 
 
 def solution(mesh):

time: 156 us -> 153 us (0.981)
  Pallas kernels: 150 us -> 145 us
    pallas_call x1, Pallas kernels: 150 us -> 145 us  [per_device(): pl.pallas_call(kernel, out_shape=(jax.ShapeDtypeStruct((ROWS + PACK, D),...]
    unnamed x6 -> x5, local copies, waits for them, and re-layouts: 1.65 us -> 4.2 us
    slice x1 -> x0, local copies, waits for them, and re-layouts: 1.89 us -> none  [per_device(): return (token_grad, grads[:H].T, grads[H:2 * H].T, grads[2 * H:])]
where the time goes in v1:
time: 153 us; the launch traced here: 152 us
  Pallas kernels  145 us (95%)
  local copies, waits for them, and re-layouts  4.2 us (3%)
  matrix products  2.23 us (1%)
    pallas_call x1, Pallas kernels, per_device(): pl.pallas_call(kernel, out_shape=(jax.ShapeDtypeStruct((ROWS + PACK, D),...  145 us
    unnamed x5, local copies, waits for them, and re-layouts  4.2 us

profile of v1, /device:TPU:2, one launch (start us, length us, event | category | flops | bytes accessed | tf_op | source)
XLA Modules:
  0.0 152.4 jit_solution(4668367400455262885)
XLA Ops:
  0.6 145.3 %shard_map.102 = (bf16[40,3072]{1,0:T(8,128)(2,1)}, bf16[40,128]{1,0:T(8,128)(2,1)}, bf16[256,384]{1,0:T(8,128)(2,1)}, bf16[256,384]{1,0:T(8,128)(2,1)}, bf16[256,384]{1,0:T(8,128)(2,1)}) custom-call(s32[2,128]{1,0:T(2,128)} %bitcast.8, f32[2,128]{1,0:T(2,128)} %bitcast.9, bf16[128,3072]{1,0:T(8,128)(2,1)} %tokens.1, bf16[128,3072]{1,0:T(8,128)(2,1)} %cot.1, ...), custom_call_target="tpu_custom_call" | custom-call | tf_op jit(solution)/shard_map/pallas_call | solution.py:552
  145.9 0.0 copy-start
  145.9 1.8 %copy.11 = bf16[384,256]{1,0:T(8,128)(2,1)} copy(bf16[384,256]{0,1:T(8,128)(2,1)} %bitcast.7) | data formatting | bytes 393216
  147.7 1.7 %copy.12 = bf16[384,256]{1,0:T(8,128)(2,1)} copy(bf16[384,256]{0,1:T(8,128)(2,1)} %bitcast.6) | data formatting | bytes 393216
  149.4 2.2 %convolution_convert_fusion = bf16[128,3072]{1,0:T(8,128)(2,1)} fusion(bf16[40,128]{1,0:T(8,128)(2,1)} %get-tuple-element.9, bf16[40,3072]{1,0:T(8,128)(2,1)} %get-tuple-element.10), kind=kOutput, calls=%fused_computation | convolution fusion | flops 31850496 | bytes 1042432 | tf_op jit(solution)/shard_map/dot_general | solution.py:566
  151.7 0.0 copy-done
  151.7 0.7 copy.14
Async XLA Ops:
  145.9 5.8 %copy-start = (bf16[256,384]{1,0:T(8,128)(2,1)S(1)}, bf16[256,384]{1,0:T(8,128)(2,1)}, u32[]{:S(2)}) copy-start(bf16[256,384]{1,0:T(8,128)(2,1)} %get-tuple-element.25) | copy-start | bytes 589828

commit v2 on v1

--- a/solution.py
+++ b/solution.py
@@ -55,6 +55,7 @@
 
 PLACE = {dz: i for i, dz in enumerate((0, 1, 7, 2, 6, 3, 5, 4))}
 EARLY = 5
+BATCHES = ((0,), (1, 7), (2, 6), (3, 5), (4,))
 
 
 def row_of(dz, dx):
@@ -114,8 +115,12 @@
             visit(0, 0, None, None, 0)
     tasks.append(Task("pick", [], first_sends, 2.0, 0, ("pick",)))
 
-    for dz in range(NZ):
-        tasks.append(Task(("main", dz), ["pick", "weights"] + by_dz[dz], [], 3.0, 3, ("main", dz)))
+    for group in BATCHES:
+        deps = ["pick", "weights"] + [k for dz in group for k in by_dz[dz]]
+        dur = 2.5 + 2.0 * len(group)
+        tasks.append(Task(("main", group[0]), deps, [], dur, 3, ("main",) + group))
+        for dz in group[1:]:
+            tasks.append(Task(("main", dz), [("main", group[0])], [], 0.0, 1))
     tasks.append(Task("weights", ["pick"], [], 0.1, 1, ("weights",)))
     task_of = {t.name: t for t in tasks}
 
@@ -412,17 +417,19 @@
 
     nt = (((1,), (1,)), ((), ()))
 
-    def main(dz):
-        rows = pl.ds(row_of(dz, 0), GROUP)
-        tail = pl.ds(row_of(dz, 0) + NX * ROWS, NX * EXTRA)
-        packed = pl.ds(pack_of(dz, 0), NX * PACK)
+    def main(*group):
+        rows = pl.ds(row_of(group[0], 0), GROUP * len(group))
+        spots = [
+            (pl.ds(row_of(dz, 0) + NX * ROWS, NX * EXTRA), pl.ds(pack_of(dz, 0), NX * PACK)) for dz in group
+        ]
         for kind, cols in (("A", CA // 2), ("B", CB // 2)):
             for tw in (0, 1):
                 for high in (0, 1):
-                    gathered[kind, tw][tail, pl.ds(high * cols, cols)] = jnp.dot(
-                        spread(high, (NX * EXTRA, NX * PACK), 0), extras[kind, tw][packed, :],
-                        preferred_element_type=F32,
-                    ).astype(BF)
+                    for tail, packed in spots:
+                        gathered[kind, tw][tail, pl.ds(high * cols, cols)] = jnp.dot(
+                            spread(high, (NX * EXTRA, NX * PACK), 0), extras[kind, tw][packed, :],
+                            preferred_element_type=F32,
+                        ).astype(BF)
         ra, rb, sa, sb = ga0[rows, :], gb0[rows, :], ga1[rows, :], gb1[rows, :]
         gate = jnp.dot(ra, wg[pl.ds(0, CA), :], preferred_element_type=F32) + jnp.dot(
             rb, wg[pl.ds(CA, CB), :], preferred_element_type=F32
@@ -448,13 +455,14 @@
             ).astype(BF)
 
         for out, c0, cols in ((pa, 0, CA // 2), (pb, CA, CB // 2)):
-            out[packed, :] = sum(
-                jnp.dot(
-                    spread(high, (NX * PACK, NX * EXTRA), 1), part[tail, pl.ds(c0 + high * cols, cols)],
-                    preferred_element_type=F32,
-                )
-                for high in (0, 1)
-            ).astype(BF)
+            for tail, packed in spots:
+                out[packed, :] = sum(
+                    jnp.dot(
+                        spread(high, (NX * PACK, NX * EXTRA), 1), part[tail, pl.ds(c0 + high * cols, cols)],
+                        preferred_element_type=F32,
+                    )
+                    for high in (0, 1)
+                ).astype(BF)
 
     def add(key, what, r0, nr, c0, nc):
         got = landing[nr, nc].at[R_SLOT[key]]
@@ -505,8 +513,9 @@
 
     def wout():
         own = shard(0, False)
-        for i, out in enumerate((g_out, u_out, d_out)):
-            out[...] = w3[pl.ds(i * H, H), own]
+        g_out[...] = jnp.transpose(w3[pl.ds(0, H), own])
+        u_out[...] = jnp.transpose(w3[pl.ds(H, H), own])
+        d_out[...] = w3[pl.ds(2 * H, H), own]
 
     run = dict(early=early, pick=pick, weights=weights, main=main, add=add, turn=turn, grad=grad,
                cadd=cadd, yadd=yadd, final=final, wout=wout)
@@ -554,7 +563,9 @@
         out_shape=(
             jax.ShapeDtypeStruct((ROWS + PACK, D), BF),
             jax.ShapeDtypeStruct((ROWS + PACK, TOK), BF),
-            *(jax.ShapeDtypeStruct((H, SH), BF) for _ in range(3)),
+            jax.ShapeDtypeStruct((SH, H), BF),
+            jax.ShapeDtypeStruct((SH, H), BF),
+            jax.ShapeDtypeStruct((H, SH), BF),
         ),
         in_specs=[vmem, vmem, vmem, vmem, anywhere, anywhere, anywhere],
         out_specs=(vmem,) * 5,
@@ -566,7 +577,7 @@
     token_grad = lax.dot_general(
         across, returned, (((0,), (0,)), ((), ())), preferred_element_type=F32
     ).astype(BF)
-    return token_grad, gate_grad.T, up_grad.T, down_grad
+    return token_grad, gate_grad, up_grad, down_grad
 
 
 def solution(mesh):

time: 153 us -> 151 us (0.987)
    unnamed x5 -> x7, local copies, waits for them, and re-layouts: 4.2 us -> 2.98 us
where the time goes in v2:
time: 151 us
  Pallas kernels  145 us (96%)
  local copies, waits for them, and re-layouts  2.98 us (2%)
  matrix products  2.28 us (2%)
    pallas_call x1, Pallas kernels, per_device(): pl.pallas_call(kernel, out_shape=(jax.ShapeDtypeStruct((ROWS + PACK, D),...  145 us

profile of v2, /device:TPU:2, one launch (start us, length us, event | category | flops | bytes accessed | tf_op | source)
XLA Modules:
  0.0 150.6 jit_solution(18218481892532214202)
XLA Ops:
  0.6 144.7 %shard_map.102 = (bf16[40,3072]{1,0:T(8,128)(2,1)}, bf16[40,128]{1,0:T(8,128)(2,1)}, bf16[384,256]{1,0:T(8,128)(2,1)}, bf16[384,256]{1,0:T(8,128)(2,1)}, bf16[256,384]{1,0:T(8,128)(2,1)}) custom-call(s32[2,128]{1,0:T(2,128)} %bitcast.4, f32[2,128]{1,0:T(2,128)} %bitcast.5, bf16[128,3072]{1,0:T(8,128)(2,1)} %tokens.1, bf16[128,3072]{1,0:T(8,128)(2,1)} %cot.1, ...), custom_call_target="tpu_custom_call" | custom-call | tf_op jit(solution)/shard_map/pallas_call | solution.py:561
  145.3 0.0 copy-start.1
  145.3 0.0 copy-start
  145.4 2.3 %convolution_convert_fusion = bf16[128,3072]{1,0:T(8,128)(2,1)} fusion(bf16[40,128]{1,0:T(8,128)(2,1)} %get-tuple-element.9, bf16[40,3072]{1,0:T(8,128)(2,1)} %get-tuple-element.10), kind=kOutput, calls=%fused_computation | convolution fusion | flops 31850496 | bytes 1042432 | tf_op jit(solution)/shard_map/dot_general | solution.py:577
  147.6 1.6 %copy.14 = bf16[384,256]{1,0:T(8,128)(2,1)} copy(bf16[384,256]{1,0:T(8,128)(2,1)} %get-tuple-element.19) | data formatting | bytes 393216
  149.3 0.0 copy-done.1
  149.3 0.7 copy.15
  149.9 0.0 copy-done
  149.9 0.7 copy.16
Async XLA Ops:
  145.3 3.9 %copy-start.1 = (bf16[384,256]{1,0:T(8,128)(2,1)S(1)}, bf16[384,256]{1,0:T(8,128)(2,1)}, u32[]{:S(2)}) copy-start(bf16[384,256]{1,0:T(8,128)(2,1)} %get-tuple-element.20) | copy-start | bytes 589828
  145.3 4.6 %copy-start = (bf16[256,384]{1,0:T(8,128)(2,1)S(1)}, bf16[256,384]{1,0:T(8,128)(2,1)}, u32[]{:S(2)}) copy-start(bf16[256,384]{1,0:T(8,128)(2,1)} %get-tuple-element.21) | copy-start | bytes 589828

commit v3 on v2

--- a/solution.py
+++ b/solution.py
@@ -55,7 +55,7 @@
 
 PLACE = {dz: i for i, dz in enumerate((0, 1, 7, 2, 6, 3, 5, 4))}
 EARLY = 5
-BATCHES = ((0,), (1, 7), (2, 6), (3, 5), (4,))
+BATCHES = ((0,), (1, 7), (2, 6), (3,), (5,), (4,))
 
 
 def row_of(dz, dx):

time: 151 us -> 150 us (level)
  Pallas kernels: 145 us -> 143 us
where the time goes in v3:
time: 150 us; the launch traced here: 149 us
  Pallas kernels  143 us (95%)
  local copies, waits for them, and re-layouts  2.98 us (2%)
  matrix products  2.29 us (2%)
    pallas_call x1, Pallas kernels, per_device(): pl.pallas_call(kernel, out_shape=(jax.ShapeDtypeStruct((ROWS + PACK, D),...  143 us

profile of v3, /device:TPU:2, one launch (start us, length us, event | category | flops | bytes accessed | tf_op | source)
XLA Modules:
  0.0 149.4 jit_solution(13092425738521105335)
XLA Ops:
  0.6 143.5 %shard_map.102 = (bf16[40,3072]{1,0:T(8,128)(2,1)}, bf16[40,128]{1,0:T(8,128)(2,1)}, bf16[384,256]{1,0:T(8,128)(2,1)}, bf16[384,256]{1,0:T(8,128)(2,1)}, bf16[256,384]{1,0:T(8,128)(2,1)}) custom-call(s32[2,128]{1,0:T(2,128)} %bitcast.4, f32[2,128]{1,0:T(2,128)} %bitcast.5, bf16[128,3072]{1,0:T(8,128)(2,1)} %tokens.1, bf16[128,3072]{1,0:T(8,128)(2,1)} %cot.1, ...), custom_call_target="tpu_custom_call" | custom-call | tf_op jit(solution)/shard_map/pallas_call | solution.py:561
  144.1 0.0 copy-start.1
  144.1 0.0 copy-start
  144.1 2.3 %convolution_convert_fusion = bf16[128,3072]{1,0:T(8,128)(2,1)} fusion(bf16[40,128]{1,0:T(8,128)(2,1)} %get-tuple-element.9, bf16[40,3072]{1,0:T(8,128)(2,1)} %get-tuple-element.10), kind=kOutput, calls=%fused_computation | convolution fusion | flops 31850496 | bytes 1042432 | tf_op jit(solution)/shard_map/dot_general | solution.py:577
  146.4 1.6 %copy.14 = bf16[384,256]{1,0:T(8,128)(2,1)} copy(bf16[384,256]{1,0:T(8,128)(2,1)} %get-tuple-element.19) | data formatting | bytes 393216
  148.0 0.0 copy-done.1
  148.0 0.7 copy.15
  148.7 0.0 copy-done
  148.7 0.7 copy.16
Async XLA Ops:
  144.1 3.9 %copy-start.1 = (bf16[384,256]{1,0:T(8,128)(2,1)S(1)}, bf16[384,256]{1,0:T(8,128)(2,1)}, u32[]{:S(2)}) copy-start(bf16[384,256]{1,0:T(8,128)(2,1)} %get-tuple-element.20) | copy-start | bytes 589828
  144.1 4.6 %copy-start = (bf16[256,384]{1,0:T(8,128)(2,1)S(1)}, bf16[256,384]{1,0:T(8,128)(2,1)}, u32[]{:S(2)}) copy-start(bf16[256,384]{1,0:T(8,128)(2,1)} %get-tuple-element.21) | copy-start | bytes 589828
